TPU v7x, 128 devices: a whole 4x4x4 slice. The times are simulated.
128 devices in a mesh: narrow: 2 (over core), wide: 64 (over z, y, x).
Axes of the slice: x: 4, y: 4, z: 4, core: 2. Of those that a mesh axis runs over, the one named last changes fastest.
Arguments:
- rows: bfloat16 [393216, 1024], P(('narrow', 'wide')), may hold values from -20 to 20
- list_ids: int32 [393216], P(('narrow', 'wide')), may hold values from 0 to 65535, as said below
- codes: int32 [393216, 64], P(('narrow', 'wide')), may hold values from 0 to 255
- row_counts: int32 [128], P(('narrow', 'wide')), may hold values from 1536 to 3072, as said below
- centroids: bfloat16 [65536, 1024], P('wide'), may hold values from -4 to 4
- old_codebook: float32 [64, 4096], replicated, may hold values from -4 to 4
Outputs:
- codebook: float32 [64, 4096], replicated
- search_table: bfloat16 [64, 4096], P('wide')
- row_error: float32 [393216], P(('narrow', 'wide'))
Inputs may be any that keep to these rules, and one draw needn't show every extreme that they name: `list_ids`: among the live passages of one device, at most 96 have lists owned by any one index w of wide (lists w * 1024 to (w + 1) * 1024 - 1), and one index of wide receives exactly 96 live passages from every device. Entries past a device's count are arbitrary. `row_counts`: one device holds exactly 3072 live passages.
All inputs are finite; a program needn't handle non-finite values.
Results may differ from a plain program's by a relative error of at most 0.00165.
Values may be sent and summed in bfloat16 or wider, within the bound.
No kernel may reach another device: no remote copies, remote signals or barrier semaphores. Data moves between devices by JAX's collectives and lax.ppermute only.
A program may use at most 192 MiB of HBM per device.

v0:
```python
import math

import jax
import jax.numpy as jnp
from jax import lax
from jax.sharding import PartitionSpec as P

K = 256


def onehot_block(piece_codes, piece_valid, words):
    match = piece_codes[:, :, None] == jnp.arange(words, dtype=jnp.int32)[None, None, :]
    return (match & piece_valid[:, None, None]).astype(jnp.bfloat16)


def gram_sums(resid, codes, valid, words):
    total_rows, width_d = resid.shape
    spaces = codes.shape[1]
    sub_width = width_d // spaces
    block_rows = math.gcd(total_rows, 512)
    groups = total_rows // block_rows

    def absorb(carry, pieces):
        piece_rows, piece_codes, piece_valid = pieces
        onehot = onehot_block(piece_codes, piece_valid, words)
        shaped = piece_rows.reshape(block_rows, spaces, sub_width)
        sums = carry[0] + jnp.einsum(
            "bmk,bms->mks", onehot, shaped, preferred_element_type=jnp.float32
        )
        counts = carry[1] + jnp.sum(onehot, axis=0, dtype=jnp.float32)
        return ((sums, counts), None)

    start = (
        jnp.zeros((spaces, words, sub_width), jnp.float32),
        jnp.zeros((spaces, words), jnp.float32),
    )
    pieces = (
        resid.reshape(groups, block_rows, width_d),
        codes.reshape(groups, block_rows, spaces),
        valid.reshape(groups, block_rows),
    )
    (sums, counts), unused = lax.scan(absorb, start, pieces)
    return (sums.reshape(spaces, words * sub_width), counts)


def row_errors(resid, codes, valid, table):
    total_rows, width_d = resid.shape
    spaces, words, sub_width = table.shape
    block_rows = math.gcd(total_rows, 512)
    groups = total_rows // block_rows

    def measure(carry, pieces):
        piece_rows, piece_codes, piece_valid = pieces
        onehot = onehot_block(piece_codes, piece_valid, words)
        decoded = jnp.einsum("bmk,mks->bms", onehot, table, preferred_element_type=jnp.float32)
        diff = piece_rows.reshape(block_rows, spaces, sub_width).astype(jnp.float32) - decoded
        err = jnp.mean(diff * diff, axis=(1, 2))
        return (carry, jnp.where(piece_valid, err, jnp.float32(0.0)))

    pieces = (
        resid.reshape(groups, block_rows, width_d),
        codes.reshape(groups, block_rows, spaces),
        valid.reshape(groups, block_rows),
    )
    unused, errs = lax.scan(measure, jnp.float32(0.0), pieces)
    return errs.reshape(total_rows)


def refit(sums, counts, previous, anchor, words):
    spaces = sums.shape[0]
    sub_width = sums.shape[1] // words
    shaped = sums.reshape(spaces, words, sub_width) + anchor * previous.reshape(
        spaces, words, sub_width
    )
    return (shaped / (counts[:, :, None] + anchor)).reshape(spaces, words * sub_width)


def body(rows, list_ids, codes, row_counts, centroids, old_codebook):
    local_rows, width_d = rows.shape
    spaces = codes.shape[1]
    words = K
    sub_width = width_d // spaces
    wide_count = lax.axis_size("wide")
    capacity = 2 * local_rows // wide_count
    slots = wide_count * capacity
    lists_owned = centroids.shape[0]
    own_index = lax.axis_index("wide")
    anchor = float(local_rows * lax.axis_size("narrow") * wide_count // (4 * words))
    position = jnp.arange(local_rows, dtype=jnp.int32)
    is_live = position < row_counts[0]
    owner_index = jnp.where(is_live, list_ids // lists_owned, wide_count)
    member = (owner_index[:, None] == jnp.arange(wide_count, dtype=jnp.int32)[None, :]).astype(
        jnp.int32
    )
    ahead = jnp.cumsum(member, axis=0) - member
    within = jnp.sum(ahead * member, axis=1)
    slot_of_row = jnp.where(is_live, owner_index * capacity + within, slots)
    source_row = jnp.full((slots + 1,), local_rows, jnp.int32).at[slot_of_row].set(position)[:slots]
    padded_lists = jnp.concatenate([list_ids, jnp.full((1,), -1, jnp.int32)])
    send_lists = padded_lists[source_row].reshape(wide_count, capacity)
    padded_rows = jnp.concatenate([rows, jnp.zeros((1, width_d), jnp.bfloat16)])
    padded_codes = jnp.concatenate([codes, jnp.zeros((1, spaces), jnp.int32)])
    send_rows = padded_rows[source_row].reshape(wide_count, capacity, width_d)
    send_codes = padded_codes[source_row].reshape(wide_count, capacity, spaces)
    got_rows, got_lists, got_codes = (
        lax.all_to_all(send_rows, "wide", split_axis=0, concat_axis=0, tiled=True),
        lax.all_to_all(send_lists, "wide", split_axis=0, concat_axis=0, tiled=True),
        lax.all_to_all(send_codes, "wide", split_axis=0, concat_axis=0, tiled=True),
    )
    flat_lists = got_lists.reshape(slots)
    valid = flat_lists >= 0
    local_list = jnp.clip(flat_lists - own_index * lists_owned, 0, lists_owned - 1)
    resid = (
        got_rows.reshape(slots, width_d).astype(jnp.float32)
        - centroids[local_list].astype(jnp.float32)
    ).astype(jnp.bfloat16)
    work_codes = got_codes.reshape(slots, spaces)
    sums, counts = gram_sums(resid, work_codes, valid, words)
    share = spaces // wide_count
    sums, counts = lax.psum((sums, counts), ("narrow", "wide"))
    codebook = refit(sums, counts, old_codebook, anchor, words)
    table_flat = codebook.astype(jnp.bfloat16)
    search_table = lax.dynamic_slice_in_dim(table_flat, own_index * share, share, 0)
    errs = row_errors(resid, work_codes, valid, table_flat.reshape(spaces, words, sub_width))
    returned = lax.all_to_all(
        errs.reshape(wide_count, capacity), "wide", split_axis=0, concat_axis=0, tiled=True
    )
    padded_errs = jnp.concatenate([returned.reshape(slots), jnp.zeros((1,), jnp.float32)])
    row_error = padded_errs[slot_of_row]
    return (codebook, search_table, row_error)


def solution(mesh):
    in_specs = (
        P(("narrow", "wide"), None),
        P(("narrow", "wide")),
        P(("narrow", "wide"), None),
        P(("narrow", "wide")),
        P("wide", None),
        P(),
    )
    out_specs = (P(), P("wide", None), P(("narrow", "wide")))
    return jax.shard_map(body, mesh=mesh, in_specs=in_specs, out_specs=out_specs, check_vma=False)
```

profile of v0, /device:TPU:1, one launch (start us, length us, event | category | flops | bytes accessed | tf_op | source)
XLA Modules:
  0.0 1014.6 jit_solution(13342150177901564543)
XLA Ops:
  9.6 31.9 %reduce-window.6 = s32[64,24,128]{2,1,0:T(8,128)S(1)} reduce-window(s32[64,24,128]{2,1,0:T(8,128)} %fusion.22, s32[]{:T(128)} %constant.33.clone.1), window={size=1x1x128 pad=0_0x0_0x127_0}, to_apply=%region_0.1 | reduce-window | flops 24969216 | bytes 1572868 | tf_op jit(solution)/shard_map/reduce-window
  47.0 11.8 %scatter_custom_fusion = s32[6145]{0:T(1024)S(1)} fusion(s32[3072]{0:T(1024)S(1)} %get-tuple-element.170, s32[3072]{0:T(1024)S(1)} %iota.22, s32[]{:T(128)} %constant.41.clone.1), kind=kCustom, calls=%fused_computation.55 | custom fusion | bytes 24584 | tf_op jit(solution)/shard_map/scatter | solution.py:98
  59.6 34.3 %gather_fusion.1 = s32[6144]{0:T(1024)S(1)} fusion(s32[3073]{0:T(1024)S(1)} %pad_add_fusion, s32[6144]{0:T(1024)S(1)} %fusion.23), kind=kCustom, calls=%fused_computation.1 | custom fusion | bytes 73728 | tf_op jit(solution)/shard_map/gather | solution.py:100
  94.6 12.0 %all-to-all-start.1 = ((s32[64,1,96]{2,1,0:T(1,128)}), s32[64,1,96]{2,1,0:T(1,128)S(1)}, u32[]{:S(2)}, u32[]{:S(2)}) async-start(s32[64,1,96]{2,1,0:T(1,128)} %all_to_all.19), calls=%async_computation.1 | async-start | bytes 65536 | tf_op jit(solution)/shard_map/all_to_all | solution.py:107
  108.2 2.7 concatenate.12
  110.8 22.3 %gather_fusion = s32[6144,64]{1,0:T(8,128)} fusion(s32[3073,64]{1,0:T(8,128)} %concatenate.12, s32[6144]{0:T(1024)S(1)} %fusion.23), kind=kCustom, calls=%fused_computation | custom fusion | bytes 3170304 | tf_op jit(solution)/shard_map/gather | solution.py:104
  133.1 3.3 copy.45
  136.5 10.0 all-to-all-start
  146.5 6.1 concatenate.14
  152.6 34.4 %gather_fusion.2 = bf16[6144,1024]{1,0:T(8,128)(2,1)} fusion(bf16[3073,1024]{1,0:T(8,128)(2,1)} %concatenate.14, s32[6144]{0:T(1024)S(1)} %fusion.23), kind=kCustom, calls=%fused_computation.2 | custom fusion | bytes 25190400 | tf_op jit(solution)/shard_map/gather | solution.py:103
  187.0 9.9 all-to-all-start.2
  197.7 26.8 %gather_fusion.3 = bf16[6144,1024]{1,0:T(8,128)(2,1)} fusion(bf16[1024,1024]{1,0:T(8,128)(2,1)S(1)} %copy-done, s32[6144]{0:T(1024)S(1)} %broadcast_clamp_fusion), kind=kCustom, calls=%fused_computation.3 | custom fusion | bytes 25190400 | tf_op jit(solution)/shard_map/gather | solution.py:115
  224.6 4.1 copy.46
  228.7 2.8 reshape_reshape.2
  231.5 2.1 copy.47
  233.6 141.1 %all-to-all-done.2 = bf16[64,96,1024]{2,1,0:T(8,128)(2,1)} async-done(((bf16[64,96,1024]{2,1,0:T(8,128)(2,1)}), bf16[64,96,1024]{2,1,0:T(8,128)(2,1)}, u32[]{:S(2)}, u32[]{:S(2)}) %all-to-all-start.2) | async-done | bytes 12582944 | tf_op jit(solution)/shard_map/all_to_all | solution.py:106
  374.6 15.4 %fusion.18 = bf16[12,512,1024]{2,1,0:T(8,128)(2,1)} fusion(bf16[12,512,1024]{2,1,0:T(8,128)(2,1)} %bitcast.69, bf16[12,512,1024]{2,1,0:T(8,128)(2,1)} %bitcast.20), kind=kLoop, calls=%fused_computation.32 | loop fusion | flops 25165824 | bytes 37748736 | tf_op jit(solution)/shard_map/convert_element_type | solution.py:116
  390.1 16.6 %copy.48 = bf16[12,512,1024]{1,2,0:T(8,128)(2,1)} copy(bf16[12,512,1024]{2,1,0:T(8,128)(2,1)} %fusion.18) | data formatting | bytes 25165824
  406.7 256.2 %while.24 = (s32[]{:T(128)}, f32[64,256,16]{1,2,0:T(8,128)}, f32[64,256]{1,0:T(8,128)S(1)}, s32[12,512,64]{1,2,0:T(8,128)}, pred[12,512]{1,0:T(8,128)(4,1)S(1)},...) while((s32[]{:T(128)}, f32[64,256,16]{1,2,0:T(8,128)}, f32[64,256]{1,0:T(8,128)S(1)}, ...), condition=%wide.region_6.7_spmd.clone, body=%wide.region_4.6_spmd.clone.sunk | while | flops 327696384 | bytes 6031468 | solution.py:42
  409.0 7.8 fusion.44
  416.8 10.1 convert_reduce_fusion.2
  429.3 9.0 fusion.44
  438.3 10.1 convert_reduce_fusion.2
  450.7 9.0 fusion.44
  459.7 10.1 convert_reduce_fusion.2
  472.1 9.0 fusion.44
  481.2 10.1 convert_reduce_fusion.2
  493.6 9.0 fusion.44
  502.6 10.1 convert_reduce_fusion.2
  515.0 9.0 fusion.44
  524.1 10.1 convert_reduce_fusion.2
  536.5 9.0 fusion.44
  545.5 10.1 convert_reduce_fusion.2
  557.9 9.0 fusion.44
  567.0 10.1 convert_reduce_fusion.2
  579.4 9.0 fusion.44
  588.4 10.1 convert_reduce_fusion.2
  600.8 9.0 fusion.44
  609.9 10.1 convert_reduce_fusion.2
  622.3 9.0 fusion.44
  631.3 10.1 convert_reduce_fusion.2
  643.7 9.0 fusion.44
  652.8 10.1 convert_reduce_fusion.2
  662.9 3.9 copy.49
  667.5 167.2 %all-reduce.5.cloned.1.call-done = (f32[64,4096]{0,1:T(8,128)}, f32[64,256]{1,0:T(8,128)}) async-done(((f32[64,4096]{0,1:T(8,128)}, f32[64,256]{1,0:T(8,128)}), (f32[64,4096]{0,1:T(8,128)}, f32[64,256]{1,0:T(8,128)})) %all-reduce.5.cloned.1.call-update) | async-done | bytes 1114128 | tf_op jit(solution)/shard_map/psum | solution.py:120
  835.6 3.3 fusion.29
  840.2 118.6 %while.23 = (s32[]{:T(128)}, f32[12,512]{1,0:T(8,128)S(1)}, pred[12,512]{1,0:T(8,128)(4,1)S(1)}, bf16[12,512,1024]{1,2,0:T(8,128)(2,1)}, s32[12,512,64]{1,2,0:T(...) while((s32[]{:T(128)}, f32[12,512]{1,0:T(8,128)S(1)}, pred[12,512]{1,0:T(8,128)(4,1)S(1)}, ...), condition=%wide.region_11.12_spmd, body=%wide.region_9.11_spmd.sunk | while | flops 287310336 | bytes 4079721 | solution.py:65
  842.7 7.5 fusion.41
  852.6 7.5 fusion.41
  862.5 7.5 fusion.41
  872.3 7.5 fusion.41
  882.2 7.5 fusion.41
  892.1 7.5 fusion.41
  901.9 7.5 fusion.41
  911.8 7.5 fusion.41
  921.7 7.5 fusion.41
  931.5 7.5 fusion.41
  941.4 7.5 fusion.41
  951.3 7.5 fusion.41
  959.6 7.7 all-to-all-start.3
  968.7 2.2 copy.56
  970.9 3.1 copy.55
  974.0 1.7 all-to-all-done.3
  977.2 30.6 %gather_fusion.4 = f32[3072]{0:T(1024)} fusion(f32[6145]{0:T(1024)S(1)} %pad_maximum_fusion, s32[3072]{0:T(1024)S(1)} %copy-done.5), kind=kCustom, calls=%fused_computation.4 | custom fusion | bytes 36864 | tf_op jit(solution)/shard_map/gather | solution.py:129
  (169 shorter events, 72.4 us)
Async XLA Ops:
  7.2 190.6 %copy-start = (bf16[1024,1024]{1,0:T(8,128)(2,1)S(1)}, bf16[1024,1024]{1,0:T(8,128)(2,1)}, u32[]{:S(2)}) copy-start(bf16[1024,1024]{1,0:T(8,128)(2,1)} %param.14) | copy-start | bytes 6291460
  59.5 47.0 %copy-start.4 = (s32[3072,64]{0,1:T(8,128)S(1)}, s32[3072,64]{0,1:T(8,128)}, u32[]{:S(2)}) copy-start(s32[3072,64]{0,1:T(8,128)} %param.12) | copy-start | bytes 2359300
  94.6 41.9 %all-to-all-start.1 = ((s32[64,1,96]{2,1,0:T(1,128)}), s32[64,1,96]{2,1,0:T(1,128)S(1)}, u32[]{:S(2)}, u32[]{:S(2)}) async-start(s32[64,1,96]{2,1,0:T(1,128)} %all_to_all.19), calls=%async_computation.1 | async-start | bytes 65536 | tf_op jit(solution)/shard_map/all_to_all | solution.py:107
  136.5 50.6 %all-to-all-start = ((s32[64,96,64]{1,2,0:T(8,128)}), s32[64,96,64]{1,2,0:T(8,128)}, u32[]{:S(2)}, u32[]{:S(2)}) async-start(s32[64,96,64]{1,2,0:T(8,128)} %copy.45), calls=%async_computation | async-start | bytes 4194304 | tf_op jit(solution)/shard_map/all_to_all | solution.py:108
  187.0 187.6 %all-to-all-start.2 = ((bf16[64,96,1024]{2,1,0:T(8,128)(2,1)}), bf16[64,96,1024]{2,1,0:T(8,128)(2,1)}, u32[]{:S(2)}, u32[]{:S(2)}) async-start(bf16[64,96,1024]{2,1,0:T(8,128)(2,1)} %bitcast.68), calls=%async_computation.2 | async-start | bytes 25165824 | tf_op jit(solution)/shard_map/all_to_all | solution.py:106
  197.0 637.7 %all-reduce.5.cloned.1.call-start = ((), (), s32[]{:S(2)}) async-start(), calls=%async_computation.4 | async-start | bytes 4325376 | tf_op jit(solution)/shard_map/psum | solution.py:120
  406.7 260.2 %copy-start.3 = (f32[64,4096]{1,0:T(8,128)S(1)}, f32[64,4096]{1,0:T(8,128)}, u32[]{:S(2)}) copy-start(f32[64,4096]{1,0:T(8,128)} %param.15) | copy-start | bytes 3145732
  662.9 3.9 copy-start.2
  840.2 137.0 %copy-start.5 = (s32[3072]{0:T(1024)S(1)}, s32[3072]{0:T(1024)}, u32[]{:S(2)}) copy-start(s32[3072]{0:T(1024)} %get-tuple-element.169) | copy-start | bytes 36868
  959.6 16.1 %all-to-all-start.3 = ((f32[64,1,96]{2,1,0:T(1,128)}), f32[64,1,96]{2,1,0:T(1,128)S(1)}, u32[]{:S(2)}, u32[]{:S(2)}) async-start(f32[64,1,96]{2,1,0:T(1,128)} %all_to_all.22), calls=%async_computation.3 | async-start | bytes 65536 | tf_op jit(solution)/shard_map/all_to_all | solution.py:125
  967.3 40.5 %copy-start.1 = (bf16[1024,1024]{1,0:T(8,128)(2,1)S(1)}, bf16[1024,1024]{1,0:T(8,128)(2,1)}, u32[]{:S(2)}) copy-start(bf16[1024,1024]{1,0:T(8,128)(2,1)} %param.14) | copy-start | bytes 6291460
Sparse Core Ops, SparseCore 0:
  667.0 167.6 all-reduce.4
where the time goes:
time: 1020 us; the launch traced here: 1010 us
  waiting for transfers between devices  310 us (30%)
  local copies, waits for them, and re-layouts  272 us (27%)
  matrix products  197 us (19%)
  other arithmetic  180 us (18%)
  starting transfers between devices  39.8 us (4%)
  between operations  15.1 us (1%)
    psum x1, waiting for transfers between devices, body(): sums, counts = lax.psum((sums, counts), ('narrow', 'wide'))  167 us
    all_to_all x1, waiting for transfers between devices, body(): lax.all_to_all(send_rows, 'wide', split_axis=0, concat_axis=0, tiled=True)  141 us
    reduce_sum x12, other arithmetic, absorb(): counts = carry[1] + jnp.sum(onehot, axis=0, dtype=jnp.float32)  122 us
    dot_general x12, matrix products, absorb(): jnp.einsum('bmk,bms->mks', onehot, shaped, preferred_element_type=jnp.flo...  107 us
    dot_general x12, matrix products, measure(): jnp.einsum('bmk,mks->bms', onehot, table, preferred_element_type=jnp.floa...  90 us
    gather x1, local copies, waits for them, and re-layouts, body(): send_rows = padded_rows[source_row].reshape(wide_count, capacity, width_d)  34.4 us
    gather x1, local copies, waits for them, and re-layouts, body(): send_lists = padded_lists[source_row].reshape(wide_count, capacity)  34.3 us
    another operation x3, other arithmetic  32.4 us
  transfers between devices with their start and end apart: 5, of which 3 were waited for; matrix products, arithmetic and copies ran while one was open for 11% of the time, Pallas kernels for 0%

commit v1 on v0

v1 whole, which is shorter than its diff:
```python
import functools

import jax
import jax.numpy as jnp
from jax import lax
from jax.experimental import pallas as pl
from jax.experimental.pallas import tpu as pltpu
from jax.sharding import PartitionSpec as P


K = 256
LOW = 4
HIGH = K // LOW
SUB = 16
LF = LOW * SUB
F32 = jnp.float32
BF16 = jnp.bfloat16
NT = (((1,), (1,)), ((), ()))


def iota(shape, dim, dtype=jnp.int32):
    return lax.broadcasted_iota(jnp.int32, shape, dim).astype(dtype)


def eye(n):
    return jnp.where(iota((n, n), 0) == iota((n, n), 1), 1.0, 0.0).astype(BF16)


def dot_nt(a, b):
    return lax.dot_general(a, b, NT, preferred_element_type=F32)


def whole(memory_space=pltpu.VMEM):
    return pl.BlockSpec(memory_space=memory_space)


def params():
    return pltpu.CompilerParams(vmem_limit_bytes=60 * 1024 * 1024)


def route_kernel(lists, count_ref, ids_ref, owner_ref, rank_ref, src_ref, lst_ref):
    n = ids_ref.shape[1]
    wide = src_ref.shape[0]
    lanes = src_ref.shape[1]
    blk = 256
    count = count_ref[0]
    tri = jnp.where(iota((blk, blk), 0) < iota((blk, blk), 1), 1.0, 0.0).astype(BF16)
    owners = iota((wide, blk), 0)
    ranks = iota((lanes, blk), 0, F32)
    acc = jnp.zeros((wide, 5 * lanes), F32)
    carry = jnp.zeros((wide, 1), F32)
    for j in range(n // blk):
        cols = slice(j * blk, (j + 1) * blk)
        ids = ids_ref[:, cols]
        pos = iota((1, blk), 1) + j * blk
        live = pos < count
        owner = ids // lists
        local = ids - owner * lists
        owner = jnp.where(live, owner, -1)
        member = jnp.where(owners == owner, 1.0, 0.0)
        member_b = member.astype(BF16)
        ahead = jnp.dot(member_b, tri, preferred_element_type=F32) + carry
        rank = jnp.sum(member * ahead, axis=0, keepdims=True)
        rank = jnp.where(live, rank, -1.0)
        carry = carry + jnp.sum(member, axis=1, keepdims=True)
        owner_ref[:, cols] = owner
        rank_ref[:, cols] = rank.astype(jnp.int32)
        hot = jnp.where(ranks == rank, 1.0, 0.0)
        stack = [hot]
        for value in (pos, local):
            high = value >> 6
            stack.append(hot * high.astype(F32))
            stack.append(hot * (value - (high << 6)).astype(F32))
        stack = jnp.concatenate(stack, axis=0).astype(BF16)
        acc = acc + dot_nt(member_b, stack)
    used = acc[:, :lanes] > 0.5
    src = acc[:, lanes : 2 * lanes] * 64.0 + acc[:, 2 * lanes : 3 * lanes]
    lst = acc[:, 3 * lanes : 4 * lanes] * 64.0 + acc[:, 4 * lanes :]
    src_ref[...] = jnp.where(used, src.astype(jnp.int32), n)
    lst_ref[...] = jnp.where(used, lst.astype(jnp.int32), 0)


def route(ids, count, wide, lists):
    n = ids.shape[0]
    return pl.pallas_call(
        functools.partial(route_kernel, lists),
        in_specs=[whole(pltpu.SMEM), whole()],
        out_specs=[whole()] * 4,
        out_shape=[
            jax.ShapeDtypeStruct((1, n), jnp.int32),
            jax.ShapeDtypeStruct((1, n), jnp.int32),
            jax.ShapeDtypeStruct((wide, 128), jnp.int32),
            jax.ShapeDtypeStruct((wide, 128), jnp.int32),
        ],
        compiler_params=params(),
        name="route",
    )(count, ids.reshape(1, n))


def pick_kernel(first, table_rows, index_ref, rows_ref, out_ref, tab, buf):
    per, cap, width = out_ref.shape
    groups = width // 128
    step = pl.program_id(0)

    @pl.when(step == 0)
    def _():
        def build(t, carry):
            r = pl.multiple_of(t * 16, 16)
            x = rows_ref[pl.ds(r, 16), :].astype(F32)
            for j in range(groups):
                tab[pl.ds(r * groups + j, 16, stride=groups), :] = x[:, j * 128 : (j + 1) * 128]
            return carry

        lax.fori_loop(0, table_rows // 16, build, 0)
        tab[table_rows * groups :, :] = jnp.zeros((groups, 128), F32)

    def fill(w, carry):
        for c in range(cap):
            i = index_ref[step * per + w, first + c]
            row = tab[pl.ds(pl.multiple_of(i * groups, groups), groups), :]
            buf[c * groups : (c + 1) * groups, :] = row
        for c in range(0, cap, 16):
            for j in range(groups):
                out_ref[w, c : c + 16, j * 128 : (j + 1) * 128] = buf[
                    pl.ds(c * groups + j, 16, stride=groups), :
                ].astype(BF16)
        return carry

    lax.fori_loop(0, per, fill, 0)


def pick(rows, index, first, cap):
    n, width = rows.shape
    wide = index.shape[0]
    per = 4
    groups = width // 128
    return pl.pallas_call(
        functools.partial(pick_kernel, first, n),
        grid_spec=pltpu.PrefetchScalarGridSpec(
            num_scalar_prefetch=1,
            grid=(wide // per,),
            in_specs=[whole()],
            out_specs=pl.BlockSpec((per, cap, width), lambda s, index: (s, 0, 0)),
            scratch_shapes=[
                pltpu.VMEM(((n + 1) * groups, 128), F32),
                pltpu.VMEM((cap * groups, 128), F32),
            ],
        ),
        out_shape=jax.ShapeDtypeStruct((wide, cap, width), BF16),
        compiler_params=params(),
        name="pick_rows",
    )(index, rows)


def codes_kernel(index_ref, count_ref, codes_ref, list_ref, out_ref, turned_ref, tab, buf):
    wide, _, lanes = out_ref.shape
    half = buf.shape[0] // 2
    n, spaces = codes_ref.shape
    codes = codes_ref[...].astype(F32).astype(BF16)
    one = eye(spaces)
    tab[0:n, :] = jnp.dot(codes, jnp.concatenate([one, one], axis=1), preferred_element_type=F32)
    tab[n:, :] = jnp.full((8, lanes), -1.0, F32)
    turned = dot_nt(one, codes)
    turned_ref[...] = jnp.where(iota((spaces, n), 1) < count_ref[0], turned, -1.0)
    left = iota((half, lanes), 1) < spaces

    def fill(w, carry):
        for c in range(2 * half):
            i = index_ref[w, c]
            buf[c : c + 1, :] = tab[pl.ds(i, 1), :]
        out_ref[w, 0:half, :] = jnp.where(left, buf[0:half, :], buf[half:, :]).astype(BF16)
        listed = jnp.broadcast_to(list_ref[pl.ds(w, 1), :], (16, lanes))
        listed = jnp.where(iota((16, lanes), 0) == 0, listed >> 6, listed & 63)
        out_ref[w, half:, :] = listed.astype(F32).astype(BF16)
        return carry

    lax.fori_loop(0, wide, fill, 0)


def pick_codes(codes, index, lists, count, cap):
    n, spaces = codes.shape
    wide = index.shape[0]
    return pl.pallas_call(
        codes_kernel,
        in_specs=[whole(pltpu.SMEM), whole(pltpu.SMEM), whole(), whole()],
        out_specs=[whole(), whole()],
        out_shape=[
            jax.ShapeDtypeStruct((wide, cap // 2 + 16, 2 * spaces), BF16),
            jax.ShapeDtypeStruct((spaces, n), F32),
        ],
        scratch_shapes=[pltpu.VMEM((n + 8, 2 * spaces), F32), pltpu.VMEM((cap, 2 * spaces), F32)],
        compiler_params=params(),
        name="pick_codes",
    )(index, count, codes, lists)


def turn_kernel(x_ref, out_ref, list_ref):
    wide, rows, lanes = x_ref.shape
    half = rows - 16
    out_ref[...] = dot_nt(eye(lanes), x_ref[:, 0:half, :].reshape(-1, lanes))

    def unpack(w, carry):
        listed = x_ref[w, half:, :].astype(F32)
        list_ref[pl.ds(w, 1), :] = (listed[0:1] * 64.0 + listed[1:2]).astype(jnp.int32)
        return carry

    lax.fori_loop(0, wide, unpack, 0)


def turn(x):
    wide, rows, lanes = x.shape
    return pl.pallas_call(
        turn_kernel,
        in_specs=[whole()],
        out_specs=[whole(), whole()],
        out_shape=[
            jax.ShapeDtypeStruct((lanes, wide * (rows - 16)), F32),
            jax.ShapeDtypeStruct((wide, lanes), jnp.int32),
        ],
        compiler_params=params(),
        name="turn_codes",
    )(x)


def split_code(row):
    high = jnp.floor(row * (1.0 / LOW))
    return high, row - LOW * high


def spread(row, rows=SUB):
    return jnp.broadcast_to(row, (rows, row.shape[1]))


def high_at(q):
    return 2 * (q % (HIGH // 2)) + q // (HIGH // 2)


def high_hot(high, t, zero, one):
    want = high_at(iota((16, high.shape[1]), 0) + t * 16).astype(F32).astype(BF16)
    return jnp.where(high == want, one, zero)


def gram_kernel(sign, counted, chunk, *refs):
    if counted:
        x_ref, codes_ref, out_ref, turned, hot, val, acc = refs
        prev_ref = None
    else:
        x_ref, codes_ref, prev_ref, out_ref, turned, hot, val, acc = refs
    lanes = x_ref.shape[-1]
    x = x_ref[...].reshape(-1, lanes)
    n = x.shape[0]
    spaces = lanes // SUB
    turned[...] = dot_nt(eye(lanes), x).astype(BF16)
    step = pl.program_id(1)
    for g in range(spaces // 4):
        acc[...] = jnp.zeros_like(acc)

        def absorb(t, carry):
            cols = pl.ds(pl.multiple_of(t * chunk, chunk), chunk)
            zero = jnp.zeros((16, chunk), BF16)
            one = jnp.ones((16, chunk), BF16)
            codes = codes_ref[:, cols]
            if counted:
                rows = iota((16, chunk), 0)
                lows = jnp.full((16, chunk), -2.0, F32)
            for i in range(4):
                m = g * 4 + i
                high, low = split_code(codes[m : m + 1, :])
                low_f = spread(low)
                high, low = spread(high).astype(BF16), low_f.astype(BF16)
                for q in range(HIGH // 16):
                    hot[i * HIGH + q * 16 : i * HIGH + (q + 1) * 16, :] = high_hot(high, q, zero, one)
                piece = turned[m * SUB : (m + 1) * SUB, cols]
                for k in range(LOW):
                    val[i * LF + k * SUB : i * LF + (k + 1) * SUB, :] = jnp.where(
                        low == jnp.full((16, chunk), k, BF16), piece, zero
                    )
                if counted:
                    lows = jnp.where(rows // LOW == i, low_f, lows)
            if counted:
                val[4 * LF :, :] = jnp.where((rows % LOW).astype(F32) == lows, 1.0, 0.0).astype(BF16)
            acc[...] += dot_nt(val[...], hot[...])
            return carry

        lax.fori_loop(0, n // chunk, absorb, 0)
        for i in range(4):
            m = g * 4 + i
            cols = slice(i * HIGH, (i + 1) * HIGH)
            top = acc[i * LF : i * LF + LF // 2, cols]
            low = acc[i * LF + LF // 2 : (i + 1) * LF, cols]
            sums = sign * jnp.concatenate([top, low], axis=1)
            if counted:
                out_ref[m, 0 : LF // 2, :] = sums
                base = 4 * LF + i * LOW
                cnt = jnp.concatenate([acc[base : base + 2, cols], acc[base + 2 : base + 4, cols]], axis=1)
                out_ref[m, LF // 2 : LF // 2 + 8, :] = jnp.concatenate([cnt, jnp.zeros((6, 2 * HIGH), F32)], axis=0)
            else:

                @pl.when(step == 0)
                def _():
                    out_ref[m, 0 : LF // 2, :] = prev_ref[m, 0 : LF // 2, :] + sums
                    out_ref[m, LF // 2 : LF // 2 + 8, :] = prev_ref[m, LF // 2 : LF // 2 + 8, :]

                @pl.when(step > 0)
                def _():
                    out_ref[m, 0 : LF // 2, :] += sums


def gram(x, codes, prev=None):
    groups, halves, cap, width = x.shape
    spaces = width // SUB
    n = groups * cap
    counted = prev is None
    chunk = 512
    assert n % chunk == 0
    state = pl.BlockSpec((8, LF // 2 + 8, 128), lambda f, h: (f, 0, 0))
    in_specs = [
        pl.BlockSpec((groups, 1, cap, 128), lambda f, h: (0, h, 0, f)),
        pl.BlockSpec((8, n), lambda f, h: (h * (spaces // 8) + f, 0)),
    ]
    rows = 4 * LF + (16 if counted else 0)
    return pl.pallas_call(
        functools.partial(gram_kernel, 1.0 if counted else -1.0, counted, chunk),
        grid=(spaces // 8, halves),
        in_specs=in_specs + ([] if counted else [state]),
        out_specs=state,
        out_shape=jax.ShapeDtypeStruct((spaces, LF // 2 + 8, 128), F32),
        scratch_shapes=[
            pltpu.VMEM((128, n), BF16),
            pltpu.VMEM((4 * HIGH, chunk), BF16),
            pltpu.VMEM((rows, chunk), BF16),
            pltpu.VMEM((rows, 4 * HIGH), F32),
        ],
        compiler_params=params(),
        name="row_sums" if counted else "centroid_sums",
    )(x, codes, *([] if counted else [prev]))


def refit_kernel(anchor, total_ref, old_ref, out_ref):
    total = total_ref[...]
    half = LF // 2
    sums = jnp.concatenate([total[0:half, 0:HIGH], total[0:half, HIGH:]], axis=0)
    counts = [total[half + k % 2 : half + k % 2 + 1, (k // 2) * HIGH : (k // 2 + 1) * HIGH] for k in range(LOW)]
    counts = jnp.concatenate([spread(c) for c in counts], axis=0)
    both = jnp.concatenate([sums, counts], axis=1)
    both = jnp.concatenate([both, jnp.zeros_like(both)], axis=0)
    both = both.T
    h = HIGH // 2
    sums = jnp.concatenate([both[0:h, 0:LF], both[h : 2 * h, 0:LF]], axis=1)
    counts = jnp.concatenate([both[2 * h : 3 * h, 0:LF], both[3 * h : 4 * h, 0:LF]], axis=1)
    out_ref[...] = (sums + anchor * old_ref[...]) / (counts + anchor)


def refit(total, old, anchor):
    return pl.pallas_call(
        functools.partial(refit_kernel, anchor),
        in_specs=[whole()] * 2,
        out_specs=whole(),
        out_shape=jax.ShapeDtypeStruct(old.shape, F32),
        compiler_params=params(),
        name="refit",
    )(total, old)


def error_kernel(rows_ref, cent_ref, codes_ref, table_ref, out_ref, blocks, resid):
    width = resid.shape[1]
    n = resid.shape[0]
    spaces = width // SUB

    @pl.when(pl.program_id(0) == 0)
    def _():
        blocks[...] = jnp.zeros_like(blocks)
        one = eye(LF)

        def build(g, carry):
            for i in range(4):
                tab = table_ref[g * 4 + i].astype(BF16)
                tab = jnp.concatenate([tab[:, 0:LF], tab[:, LF:]], axis=0)
                blocks[g, i * LF : (i + 1) * LF, i * HIGH : (i + 1) * HIGH] = dot_nt(one, tab).astype(BF16)
            return carry

        lax.fori_loop(0, spaces // 4, build, 0)

    rows = rows_ref[...].reshape(n, width).astype(F32)
    cent = cent_ref[...].reshape(n, width).astype(F32)
    resid[...] = (rows - cent).astype(BF16)
    one = eye(128)
    zero16 = jnp.zeros((16, n), BF16)
    one16 = jnp.ones((16, n), BF16)

    def part(f, acc):
        turned = dot_nt(one, resid[:, pl.ds(pl.multiple_of(f * 128, 128), 128)])
        codes = codes_ref[pl.ds(pl.multiple_of(f * 8, 8), 8), :]
        for g in range(2):
            hot, lows = [], []
            for i in range(4):
                m = g * 4 + i
                high, low = split_code(codes[m : m + 1, :])
                lows.append(low)
                high = spread(high).astype(BF16)
                for q in range(HIGH // 16):
                    hot.append(high_hot(high, q, zero16, one16))
            hot = jnp.concatenate(hot, axis=0)
            words = jnp.dot(blocks[f * 2 + g], hot, preferred_element_type=F32)
            for i in range(4):
                m = g * 4 + i
                low = spread(lows[i])
                word = words[i * LF + (LOW - 1) * SUB : (i + 1) * LF, :]
                for k in range(LOW - 1):
                    word = jnp.where(low == float(k), words[i * LF + k * SUB : i * LF + (k + 1) * SUB, :], word)
                diff = turned[m * SUB : (m + 1) * SUB, :] - word
                acc = acc + diff * diff
        return acc

    acc = lax.fori_loop(0, width // 128, part, jnp.zeros((SUB, n), F32))
    out_ref[...] = jnp.sum(acc, axis=0, keepdims=True) * (1.0 / width)


def errors(rows, cent, codes, table, half):
    wide, cap, width = rows.shape
    spaces = width // SUB
    per = 8
    n = per * cap
    return pl.pallas_call(
        error_kernel,
        grid=(wide // per,),
        in_specs=[
            pl.BlockSpec((per, cap, width), lambda s: (s, 0, 0)),
            pl.BlockSpec((per, 1, cap, width), lambda s: (s, half, 0, 0)),
            pl.BlockSpec((spaces, n), lambda s: (half, s)),
            whole(),
        ],
        out_specs=pl.BlockSpec((1, n), lambda s: (0, s)),
        out_shape=jax.ShapeDtypeStruct((1, wide * cap), F32),
        scratch_shapes=[
            pltpu.VMEM((spaces // 4, 4 * LF, 4 * HIGH), BF16),
            pltpu.VMEM((n, width), BF16),
        ],
        compiler_params=params(),
        name="errors",
    )(rows, cent, codes, table)


def home_kernel(owner_ref, rank_ref, first_ref, second_ref, out_ref):
    wide, cap = first_ref.shape
    n = owner_ref.shape[1]
    owner = owner_ref[...]
    rank = rank_ref[...]
    member = jnp.where(iota((wide, n), 0) == owner, 1.0, 0.0).astype(BF16)
    member = jnp.concatenate([member] * 3, axis=0)
    one = eye(cap)
    total = jnp.zeros((1, n), F32)
    for h, ref in enumerate((first_ref, second_ref)):
        left = ref[...]
        pieces = []
        for _ in range(3):
            piece = left.astype(BF16)
            left = left - piece.astype(F32)
            pieces.append(dot_nt(one, piece))
        pieces = jnp.concatenate(pieces, axis=1).astype(BF16)
        slots = jnp.dot(pieces, member, preferred_element_type=F32)
        mine = iota((cap, n), 0) + h * cap == rank
        total = total + jnp.sum(jnp.where(mine, slots, 0.0), axis=0, keepdims=True)
    out_ref[...] = total


def bring_home(owner, rank, first, second):
    n = owner.shape[1]
    return pl.pallas_call(
        home_kernel,
        in_specs=[whole()] * 4,
        out_specs=whole(),
        out_shape=jax.ShapeDtypeStruct((1, n), F32),
        compiler_params=params(),
        name="bring_home",
    )(owner, rank, first, second)


def exchange(x):
    return lax.all_to_all(x, "wide", split_axis=0, concat_axis=0, tiled=True)


def swap(x, bit):
    if bit is None:
        return lax.ppermute(x, "narrow", [(0, 1), (1, 0)])
    return lax.ppermute(x, "wide", [(i, i ^ (1 << bit)) for i in range(lax.axis_size("wide"))])


def share_bits():
    last = lax.axis_size("wide").bit_length() - 2
    order = sorted(range(last + 1), key=lambda b: (b % 2, -b))
    return [None] + order[:-1], order[-1]


def own_bit(bit):
    return lax.axis_index("narrow") if bit is None else (lax.axis_index("wide") >> bit) & 1


def reduce_shares(x):
    bits, rest = share_bits()
    for bit in bits:
        x = x.reshape((2, x.shape[0] // 2) + x.shape[1:])
        here = own_bit(bit)
        away = lax.dynamic_index_in_dim(x, 1 - here, 0, keepdims=False)
        x = lax.dynamic_index_in_dim(x, here, 0, keepdims=False) + swap(away, bit)
    return x + swap(x, rest)


def gather_shares(x):
    bits, _ = share_bits()
    for bit in reversed(bits):
        other = swap(x, bit)
        x = jnp.where(own_bit(bit) == 0, jnp.stack([x, other]), jnp.stack([other, x]))
        x = x.reshape((-1,) + x.shape[2:])
    return x


def own_share():
    share = jnp.int32(0)
    for bit in share_bits()[0]:
        share = share * 2 + own_bit(bit)
    return share


def refit_step(rows, list_ids, codes, row_counts, centroids, old_codebook):
    local_rows, width = rows.shape
    spaces = codes.shape[1]
    wide = lax.axis_size("wide")
    cap = 2 * local_rows // wide
    half = cap // 2
    lists = centroids.shape[0]
    own = lax.axis_index("wide")
    anchor = float(local_rows * lax.axis_size("narrow") * wide // (4 * K))

    owner, rank, src, lst = route(list_ids, row_counts, wide, lists)
    sent_codes, codes_local = pick_codes(codes, src, lst, row_counts, cap)
    got_codes = exchange(sent_codes)
    got_first = exchange(pick(rows, src, 0, half))
    got_second = exchange(pick(rows, src, half, half))

    sums = gram(rows.reshape(1, 1, local_rows, width), codes_local)
    codes_slots, got_lists = turn(got_codes)
    cent = pick(centroids, got_lists, 0, cap).reshape(wide, 2, half, width)
    sums = gram(cent, codes_slots, sums)
    mine = reduce_shares(sums)
    old = lax.dynamic_slice_in_dim(old_codebook, own_share(), 1, 0).reshape(K * SUB // 128, 128)
    word = refit(mine[0], old, anchor)
    book = gather_shares(word[None])
    codebook = book.reshape(spaces, K * SUB)
    search_table = lax.dynamic_slice_in_dim(codebook, own, 1, 0).astype(BF16)

    err_first = errors(got_first, cent, codes_slots, book, 0)
    err_second = errors(got_second, cent, codes_slots, book, 1)
    back_first = exchange(err_first.reshape(wide, half))
    back_second = exchange(err_second.reshape(wide, half))
    row_error = bring_home(owner, rank, back_first, back_second).reshape(local_rows)
    return (codebook, search_table, row_error)


def solution(mesh):
    in_specs = (
        P(("narrow", "wide"), None),
        P(("narrow", "wide")),
        P(("narrow", "wide"), None),
        P(("narrow", "wide")),
        P("wide", None),
        P(),
    )
    out_specs = (P(), P("wide", None), P(("narrow", "wide")))
    return jax.shard_map(refit_step, mesh=mesh, in_specs=in_specs, out_specs=out_specs, check_vma=False)
```

time: 1020 us -> 448 us (0.44)
  local copies, waits for them, and re-layouts: 272 us -> 9.35 us
  Pallas kernels: 0 us -> 234 us
  waiting for transfers between devices: 310 us -> 104 us
  matrix products: 197 us -> 0 us
  other arithmetic: 180 us -> 7.35 us
  starting transfers between devices: 39.8 us -> 88.4 us
  between operations: 15.1 us -> 1.56 us
    pallas_call x0 -> x12, Pallas kernels: none -> 234 us  [the longest x2 103 us: gram(): pl.pallas_call(functools.partial(gram_kernel, 1.0 if counted else -1.0, c...]
    dot_general x24 -> x0, matrix products: 197 us -> none  [the longest x12 107 us: absorb(): jnp.einsum('bmk,bms->mks', onehot, shaped, preferred_element_type=jnp.flo...]
    psum x1 -> x0, waiting for transfers between devices: 167 us -> none  [body(): sums, counts = lax.psum((sums, counts), ('narrow', 'wide'))]
    gather x5 -> x0, local copies, waits for them, and re-layouts: 148 us -> none  [the longest x1 34.4 us: body(): send_rows = padded_rows[source_row].reshape(wide_count, capacity, width_d)]
    reduce_sum x13 -> x0, other arithmetic: 122 us -> none  [the longest x12 122 us: absorb(): counts = carry[1] + jnp.sum(onehot, axis=0, dtype=jnp.float32)]
    all_to_all x4 -> x5, waiting for transfers between devices: 143 us -> 73.4 us  [exchange(): return lax.all_to_all(x, 'wide', split_axis=0, concat_axis=0, tiled=True)]
    ppermute x0 -> x13, starting transfers between devices: none -> 35.4 us  [the longest x11 22.1 us: swap(): lax.ppermute(x, 'wide', [(i, i ^ 1 << bit) for i in range(lax.axis_size('...]
    dynamic_slice x49 -> x1, local copies, waits for them, and re-layouts: 33.1 us -> 0.62 us  [refit_step(): lax.dynamic_slice_in_dim(old_codebook, own_share(), 1, 0)]
  transfers between devices with their start and end apart: 5 -> 18, of which waited for: 3 -> 16; matrix products, arithmetic and copies ran while one was open for 11% -> 2% of each run, Pallas kernels for 0% -> 49%
where the time goes in v1:
time: 448 us; the launch traced here: 445 us
  Pallas kernels  234 us (52%)
  waiting for transfers between devices  104 us (23%)
  starting transfers between devices  88.4 us (20%)
  local copies, waits for them, and re-layouts  9.35 us (2%)
  other arithmetic  7.35 us (2%)
    pallas_call x2, Pallas kernels, gram(): pl.pallas_call(functools.partial(gram_kernel, 1.0 if counted else -1.0, c...  103 us
    all_to_all x5, waiting for transfers between devices, exchange(): return lax.all_to_all(x, 'wide', split_axis=0, concat_axis=0, tiled=True)  73.4 us
    pallas_call x2, Pallas kernels, errors(): pl.pallas_call(error_kernel, grid=(wide // per,), in_specs=[pl.BlockSpec(...  62 us
    all_to_all x5, starting transfers between devices, exchange(): return lax.all_to_all(x, 'wide', split_axis=0, concat_axis=0, tiled=True)  52.9 us
    pallas_call x3, Pallas kernels, pick(): pl.pallas_call(functools.partial(pick_kernel, first, n), grid_spec=pltpu....  48.9 us
    ppermute x11, waiting for transfers between devices, swap(): lax.ppermute(x, 'wide', [(i, i ^ 1 << bit) for i in range(lax.axis_size('...  27.7 us
    ppermute x11, starting transfers between devices, swap(): lax.ppermute(x, 'wide', [(i, i ^ 1 << bit) for i in range(lax.axis_size('...  22.1 us
    ppermute x2, starting transfers between devices, swap(): return lax.ppermute(x, 'narrow', [(0, 1), (1, 0)])  13.3 us
  transfers between devices with their start and end apart: 18, of which 16 were waited for; matrix products, arithmetic and copies ran while one was open for 2% of the time, Pallas kernels for 49%

profile of v1, /device:TPU:1, one launch (start us, length us, event | category | flops | bytes accessed | tf_op | source)
XLA Modules:
  0.0 445.4 jit_solution(14565209333159663049)
XLA Ops:
  0.6 0.0 copy-start
  1.4 2.8 copy.11.codes_ref
  4.2 4.5 %route.1 = (s32[1,3072]{1,0:T(1,128)}, s32[1,3072]{1,0:T(1,128)}, s32[64,128]{1,0:T(8,128)}, s32[64,128]{1,0:T(8,128)}) custom-call(s32[1]{0:T(128)S(6)} %copy.17.count_ref, s32[1,3072]{1,0:T(1,128)} %bitcast.98), custom_call_target="tpu_custom_call" | custom-call | tf_op jit(solution)/shard_map/route/pallas_call | solution.py:85
  8.6 9.3 %pick_codes.1 = (bf16[64,64,128]{2,1,0:T(8,128)(2,1)}, f32[64,3072]{1,0:T(8,128)}) custom-call(s32[64,128]{1,0:T(8,128)} %get-tuple-element.11.index_ref, s32[1]{0:T(128)S(6)} %copy.17.count_ref, s32[3072,64]{1,0:T(8,128)} %copy.11.codes_ref, s32[64,128]{1,0:T(8,128)} %get-tuple-element.12.list_ref), custom_call_target="tpu_custom_call" | custom-call | tf_op jit(solution)/shard_map/pick_codes/pallas_call | solution.py:183
  17.9 12.0 %all-to-all-start = ((bf16[64,64,128]{2,1,0:T(8,128)(2,1)}), bf16[64,64,128]{2,1,0:T(8,128)(2,1)S(1)}, u32[]{:S(2)}, u32[]{:S(2)}) async-start(bf16[64,64,128]{2,1,0:T(8,128)(2,1)} %get-tuple-element.13), calls=%async_computation | async-start | bytes 2097152 | tf_op jit(solution)/shard_map/all_to_all | solution.py:480
  29.9 16.1 %pick_rows.5 = bf16[64,48,1024]{2,1,0:T(8,128)(2,1)} custom-call(s32[64,128]{1,0:T(8,128)} %get-tuple-element.11.index_ref, bf16[3072,1024]{1,0:T(8,128)(2,1)} %rows_ref.5), custom_call_target="tpu_custom_call" | custom-call | tf_op jit(solution)/shard_map/pick_rows/pallas_call | solution.py:137
  46.0 1.6 all-to-all-done.x_ref
  47.6 1.0 copy-done.2
  48.6 8.4 %all-to-all-start.3 = ((bf16[64,48,1024]{2,1,0:T(8,128)(2,1)}), bf16[64,48,1024]{2,1,0:T(8,128)(2,1)}, u32[]{:S(2)}, u32[]{:S(2)}) async-start(bf16[64,48,1024]{2,1,0:T(8,128)(2,1)} %pick_rows.5), calls=%async_computation.3 | async-start | bytes 12582912 | tf_op jit(solution)/shard_map/all_to_all | solution.py:480
  56.9 16.0 %pick_rows.4 = bf16[64,48,1024]{2,1,0:T(8,128)(2,1)} custom-call(s32[64,128]{1,0:T(8,128)} %get-tuple-element.11.index_ref, bf16[3072,1024]{1,0:T(8,128)(2,1)} %rows_ref.5), custom_call_target="tpu_custom_call" | custom-call | tf_op jit(solution)/shard_map/pick_rows/pallas_call | solution.py:137
  73.0 63.9 %all-to-all-done.3.rows_ref = bf16[64,48,1024]{2,1,0:T(8,128)(2,1)} async-done(((bf16[64,48,1024]{2,1,0:T(8,128)(2,1)}), bf16[64,48,1024]{2,1,0:T(8,128)(2,1)}, u32[]{:S(2)}, u32[]{:S(2)}) %all-to-all-start.3) | async-done | bytes 6291488 | tf_op jit(solution)/shard_map/all_to_all | solution.py:480
  136.9 12.8 %all-to-all-start.1 = ((bf16[64,48,1024]{2,1,0:T(8,128)(2,1)}), bf16[64,48,1024]{2,1,0:T(8,128)(2,1)}, u32[]{:S(2)}, u32[]{:S(2)}) async-start(bf16[64,48,1024]{2,1,0:T(8,128)(2,1)} %pick_rows.4), calls=%async_computation.1 | async-start | bytes 12582912 | tf_op jit(solution)/shard_map/all_to_all | solution.py:480
  149.7 33.2 %row_sums.1.refs_2_ = f32[64,40,128]{2,1,0:T(8,128)} custom-call(bf16[1,1,3072,1024]{3,2,1,0:T(8,128)(2,1)} %bitcast.61, f32[64,3072]{1,0:T(8,128)} %get-tuple-element.16.refs_1_), custom_call_target="tpu_custom_call" | custom-call | tf_op jit(solution)/shard_map/row_sums/pallas_call | solution.py:322
  182.9 3.3 turn_codes.1
  186.2 16.8 %pick_rows.3 = bf16[64,96,1024]{2,1,0:T(8,128)(2,1)} custom-call(s32[64,128]{1,0:T(8,128)} %get-tuple-element.14.index_ref, bf16[1024,1024]{1,0:T(8,128)(2,1)} %rows_ref.3), custom_call_target="tpu_custom_call" | custom-call | tf_op jit(solution)/shard_map/pick_rows/pallas_call | solution.py:137
  202.9 69.5 %centroid_sums.1 = f32[64,40,128]{2,1,0:T(8,128)} custom-call(bf16[64,2,48,1024]{3,2,1,0:T(8,128)(2,1)} %bitcast.58, f32[128,3072]{1,0:T(8,128)} %get-tuple-element.15.refs_1_.codes_ref, f32[64,40,128]{2,1,0:T(8,128)} %row_sums.1.refs_2_), custom_call_target="tpu_custom_call" | custom-call | tf_op jit(solution)/shard_map/centroid_sums/pallas_call | solution.py:322
  272.4 1.1 dynamic-slice_bitcast_fusion
  273.6 1.1 collective-permute-start
  274.7 1.7 collective-permute-done
  276.4 1.2 bitcast_add_fusion
  277.6 1.3 collective-permute-start.1
  278.9 7.7 %collective-permute-done.1 = f32[16,40,128]{2,1,0:T(8,128)S(1)} collective-permute-done((f32[16,40,128]{2,1,0:T(8,128)S(1)}, f32[16,40,128]{2,1,0:T(8,128)S(1)}, u32[]{:S(2)}, u32[]{:S(2)}) %collective-permute-start.1) | collective-permute-done | bytes 327712 | tf_op jit(solution)/shard_map/ppermute | solution.py:486
  286.7 1.3 collective-permute-start.2
  288.0 3.3 collective-permute-done.2
  291.3 1.3 collective-permute-start.3
  292.6 2.1 collective-permute-done.3
  294.7 2.9 collective-permute-start.4
  297.6 1.5 collective-permute-done.4
  299.2 2.8 collective-permute-start.5
  302.0 1.4 collective-permute-done.5
  303.4 2.7 collective-permute-start.6
  306.1 0.6 constant_dynamic-slice_fusion
  306.8 0.8 collective-permute-done.6
  307.6 0.6 add_bitcast_fusion.total_ref
  308.2 1.6 refit.1
  309.8 2.7 collective-permute-start.7
  312.5 1.6 collective-permute-done.7
  314.1 0.8 maximum_select_fusion.6
  314.9 2.8 collective-permute-start.8
  317.7 0.8 maximum_select_fusion.5
  318.5 0.7 collective-permute-done.8
  319.2 1.3 collective-permute-start.9
  320.5 1.9 collective-permute-done.9
  322.4 1.3 collective-permute-start.10
  323.7 2.6 collective-permute-done.10
  326.3 1.5 collective-permute-start.11
  327.8 4.3 collective-permute-done.11
  332.1 12.2 %collective-permute-start.12 = (f32[32,32,128]{2,1,0:T(8,128)S(1)}, f32[32,32,128]{2,1,0:T(8,128)S(1)}, u32[]{:S(2)}, u32[]{:S(2)}) collective-permute-start(f32[32,32,128]{2,1,0:T(8,128)S(1)} %bitcast.69), channel_id=1, source_target_pairs={{0,64},{64,0},{1,65},{65,1},{2,66},{66,2},{3,67},{67,3},{4,68},{68... | collective-permute-start | bytes 1572872 | tf_op jit(solution)/shard_map/ppermute | solution.py:485
  344.4 1.5 collective-permute-done.12
  345.9 1.1 maximum_select_fusion
  347.0 31.0 %errors.3 = f32[1,3072]{1,0:T(1,128)} custom-call(bf16[64,48,1024]{2,1,0:T(8,128)(2,1)} %all-to-all-done.3.rows_ref, bf16[64,2,48,1024]{3,2,1,0:T(8,128)(2,1)} %bitcast.59, f32[128,3072]{1,0:T(8,128)} %get-tuple-element.15.refs_1_.codes_ref, f32[64,32,128]{2,1,0:T(8,128)} %bitcast.62), custom_call_target="tpu_custom_call" | custom-call | tf_op jit(solution)/shard_map/errors/pallas_call | solution.py:424
  377.9 0.5 broadcast.70
  378.4 1.4 reduce.7
  379.8 0.7 all_to_all.29
  380.5 10.0 %all-to-all-start.4 = ((f32[64,1,48]{2,1,0:T(1,128)}), f32[64,1,48]{2,1,0:T(1,128)S(1)}, u32[]{:S(2)}, u32[]{:S(2)}) async-start(f32[64,1,48]{2,1,0:T(1,128)} %bitcast.39), calls=%async_computation.4 | async-start | bytes 65536 | tf_op jit(solution)/shard_map/all_to_all | solution.py:480
  390.5 0.6 copy.16
  391.2 31.0 %errors.2 = f32[1,3072]{1,0:T(1,128)} custom-call(bf16[64,48,1024]{2,1,0:T(8,128)(2,1)} %all-to-all-done.1.rows_ref, bf16[64,2,48,1024]{3,2,1,0:T(8,128)(2,1)} %bitcast.60, f32[128,3072]{1,0:T(8,128)} %get-tuple-element.15.refs_1_.codes_ref, f32[64,32,128]{2,1,0:T(8,128)} %bitcast.63), custom_call_target="tpu_custom_call" | custom-call | tf_op jit(solution)/shard_map/errors/pallas_call | solution.py:424
  422.2 1.4 reduce.6
  423.6 0.7 all_to_all.25
  424.3 9.8 %all-to-all-start.2 = ((f32[64,1,48]{2,1,0:T(1,128)}), f32[64,1,48]{2,1,0:T(1,128)S(1)}, u32[]{:S(2)}, u32[]{:S(2)}) async-start(f32[64,1,48]{2,1,0:T(1,128)} %bitcast.37), calls=%async_computation.2 | async-start | bytes 65536 | tf_op jit(solution)/shard_map/all_to_all | solution.py:480
  434.1 0.6 dynamic-slice_convert_fusion
  434.7 7.8 %all-to-all-done.2 = f32[64,1,48]{2,1,0:T(1,128)S(1)} async-done(((f32[64,1,48]{2,1,0:T(1,128)}), f32[64,1,48]{2,1,0:T(1,128)S(1)}, u32[]{:S(2)}, u32[]{:S(2)}) %all-to-all-start.2) | async-done | bytes 12320 | tf_op jit(solution)/shard_map/all_to_all | solution.py:480
  442.5 0.6 copy-done.5
  443.1 2.3 bring_home.1
  (25 shorter events, 0.3 us)
Async XLA Ops:
  0.6 305.5 %copy-start = (f32[64,4096]{1,0:T(8,128)S(1)}, f32[64,4096]{1,0:T(8,128)}, u32[]{:S(2)}) copy-start(f32[64,4096]{1,0:T(8,128)} %param.11) | copy-start | bytes 3145732
  17.9 29.7 %all-to-all-start = ((bf16[64,64,128]{2,1,0:T(8,128)(2,1)}), bf16[64,64,128]{2,1,0:T(8,128)(2,1)S(1)}, u32[]{:S(2)}, u32[]{:S(2)}) async-start(bf16[64,64,128]{2,1,0:T(8,128)(2,1)} %get-tuple-element.13), calls=%async_computation | async-start | bytes 2097152 | tf_op jit(solution)/shard_map/all_to_all | solution.py:480
  47.6 1.0 copy-start.2
  48.6 88.3 %all-to-all-start.3 = ((bf16[64,48,1024]{2,1,0:T(8,128)(2,1)}), bf16[64,48,1024]{2,1,0:T(8,128)(2,1)}, u32[]{:S(2)}, u32[]{:S(2)}) async-start(bf16[64,48,1024]{2,1,0:T(8,128)(2,1)} %pick_rows.5), calls=%async_computation.3 | async-start | bytes 12582912 | tf_op jit(solution)/shard_map/all_to_all | solution.py:480
  136.9 243.6 %all-to-all-start.1 = ((bf16[64,48,1024]{2,1,0:T(8,128)(2,1)}), bf16[64,48,1024]{2,1,0:T(8,128)(2,1)}, u32[]{:S(2)}, u32[]{:S(2)}) async-start(bf16[64,48,1024]{2,1,0:T(8,128)(2,1)} %pick_rows.4), calls=%async_computation.1 | async-start | bytes 12582912 | tf_op jit(solution)/shard_map/all_to_all | solution.py:480
  273.6 2.8 collective-permute-start
  277.6 9.0 %collective-permute-start.1 = (f32[16,40,128]{2,1,0:T(8,128)S(1)}, f32[16,40,128]{2,1,0:T(8,128)S(1)}, u32[]{:S(2)}, u32[]{:S(2)}) collective-permute-start(f32[16,40,128]{2,1,0:T(8,128)S(1)} %dynamic-slice_bitcast_fusion.1), channel_id=1, source_target_pairs={{0,16},{1,17},{2,18},{3,19},{4,20},{5,21},{6,22},{7,23},{8,24},{9,... | collective-permute-start | bytes 983048 | tf_op jit(solution)/shard_map/ppermute | solution.py:486
  286.7 4.6 %collective-permute-start.2 = (f32[8,40,128]{2,1,0:T(8,128)S(1)}, f32[8,40,128]{2,1,0:T(8,128)S(1)}, u32[]{:S(2)}, u32[]{:S(2)}) collective-permute-start(f32[8,40,128]{2,1,0:T(8,128)S(1)} %dynamic-slice_bitcast_fusion.2), channel_id=1, source_target_pairs={{0,4},{1,5},{2,6},{3,7},{4,0},{5,1},{6,2},{7,3},{8,12},{9,13},{10,... | collective-permute-start | bytes 491528 | tf_op jit(solution)/shard_map/ppermute | solution.py:486
  291.3 3.4 collective-permute-start.3
  294.7 4.4 collective-permute-start.4
  299.2 4.2 collective-permute-start.5
  303.4 4.1 collective-permute-start.6
  309.8 4.3 collective-permute-start.7
  314.9 4.3 collective-permute-start.8
  319.2 3.2 collective-permute-start.9
  322.4 3.9 collective-permute-start.10
  326.3 5.8 %collective-permute-start.11 = (f32[16,32,128]{2,1,0:T(8,128)S(1)}, f32[16,32,128]{2,1,0:T(8,128)S(1)}, u32[]{:S(2)}, u32[]{:S(2)}) collective-permute-start(f32[16,32,128]{2,1,0:T(8,128)S(1)} %bitcast.75), channel_id=1, source_target_pairs={{0,16},{1,17},{2,18},{3,19},{4,20},{5,21},{6,22},{7,23},{8,24},{9,... | collective-permute-start | bytes 786440 | tf_op jit(solution)/shard_map/ppermute | solution.py:486
  332.1 13.8 %collective-permute-start.12 = (f32[32,32,128]{2,1,0:T(8,128)S(1)}, f32[32,32,128]{2,1,0:T(8,128)S(1)}, u32[]{:S(2)}, u32[]{:S(2)}) collective-permute-start(f32[32,32,128]{2,1,0:T(8,128)S(1)} %bitcast.69), channel_id=1, source_target_pairs={{0,64},{64,0},{1,65},{65,1},{2,66},{66,2},{3,67},{67,3},{4,68},{68... | collective-permute-start | bytes 1572872 | tf_op jit(solution)/shard_map/ppermute | solution.py:485
  347.0 43.6 %copy-start.1 = (f32[2,32,32,128]{3,2,1,0:T(8,128)S(1)}, f32[2,32,32,128]{3,2,1,0:T(8,128)}, u32[]{:S(2)}) copy-start(f32[2,32,32,128]{3,2,1,0:T(8,128)} %maximum_select_fusion) | copy-start | bytes 3145732
  380.5 43.7 %all-to-all-start.4 = ((f32[64,1,48]{2,1,0:T(1,128)}), f32[64,1,48]{2,1,0:T(1,128)S(1)}, u32[]{:S(2)}, u32[]{:S(2)}) async-start(f32[64,1,48]{2,1,0:T(1,128)} %bitcast.39), calls=%async_computation.4 | async-start | bytes 65536 | tf_op jit(solution)/shard_map/all_to_all | solution.py:480
  391.2 42.9 %copy-start.3 = (f32[8,8,32,128]{3,1,2,0:T(8,128)}, f32[8,8,32,128]{3,1,2,0:T(8,128)S(1)}, u32[]{:S(2)}) copy-start(f32[8,8,32,128]{3,1,2,0:T(8,128)S(1)} %copy.16) | copy-start | bytes 3145732
  424.3 18.2 %copy-start.4 = (f32[64,1,48]{2,1,0:T(1,128)}, f32[64,1,48]{2,1,0:T(1,128)S(1)}, u32[]{:S(2)}) copy-start(f32[64,1,48]{2,1,0:T(1,128)S(1)} %all-to-all-done.4) | copy-start | bytes 36868
  424.3 18.2 %all-to-all-start.2 = ((f32[64,1,48]{2,1,0:T(1,128)}), f32[64,1,48]{2,1,0:T(1,128)S(1)}, u32[]{:S(2)}, u32[]{:S(2)}) async-start(f32[64,1,48]{2,1,0:T(1,128)} %bitcast.37), calls=%async_computation.2 | async-start | bytes 65536 | tf_op jit(solution)/shard_map/all_to_all | solution.py:480
  442.5 0.6 copy-start.5
